TPU v7x, 32 devices: a whole 2x2x4 slice. The times are simulated.
32 devices in a mesh: row: 4 (over y, x), col: 8 (over z, core).
Axes of the slice: x: 2, y: 2, z: 4, core: 2. Of those that a mesh axis runs over, the one named last changes fastest.
Arguments:
- image: bfloat16 [64, 256, 768], P('row', 'col'), may hold values from -6 to 6
- conv_taps: float32 [9, 768], replicated, may hold values from -0.5 to 0.5
- w_query: bfloat16 [768, 768], replicated, may hold values from -0.21875 to 0.21875
- w_key: bfloat16 [768, 768], replicated, may hold values from -0.21875 to 0.21875
- w_value: bfloat16 [768, 768], replicated, may hold values from -0.21875 to 0.21875
- w_out: bfloat16 [768, 768], replicated, may hold values from -0.21875 to 0.21875
- grad_out: bfloat16 [64, 256, 768], P('row', 'col'), may hold values from -6 to 6
Outputs:
- grad_image: bfloat16 [64, 256, 768], P('row', 'col')
- grad_weights: float32 [768, 3072], P(None, 'col')
- grad_conv: float32 [9, 768], P(None, 'col')
All inputs are finite; a program needn't handle non-finite values.
Results may differ from a plain program's by a relative error of at most 0.022.
Values may be sent and summed in bfloat16 or wider, within the bound.
A program may use at most 128 MiB of HBM per device.

v0:
```python
from functools import partial
import math
import jax
import jax.numpy as jnp
from jax import lax
from jax.sharding import PartitionSpec as P

HEADS = 12
HD = 64
POOL = 8
EPSILON = 1e-05


def with_halo(cells, sides, width):
    for axis, dim in sides:
        count = lax.axis_size(axis)
        ends = count - 1
        head = lax.slice_in_dim(cells, 0, width, axis=dim)
        tail = lax.slice_in_dim(cells, cells.shape[dim] - width, cells.shape[dim], axis=dim)
        cells = jnp.concatenate(
            [
                lax.ppermute(tail, axis, [(i, (i + 1) % count) for i in range(ends)]),
                cells,
                lax.ppermute(head, axis, [((i + 1) % count, i) for i in range(ends)]),
            ],
            axis=dim,
        )
    return cells


def contract_first(left, right):
    return lax.dot_general(
        left, right, (((0,), (0,)), ((), ())), preferred_element_type=jnp.float32
    )


def contract_last(left, right):
    return lax.dot_general(
        left, right, (((1,), (1,)), ((), ())), preferred_element_type=jnp.float32
    )


def exact_first(left, right):
    return lax.dot_general(
        left,
        right,
        (((0,), (0,)), ((), ())),
        precision=lax.Precision.HIGHEST,
        preferred_element_type=jnp.float32,
    )


def exact_last(left, right):
    return lax.dot_general(
        left,
        right,
        (((1,), (1,)), ((), ())),
        precision=lax.Precision.HIGHEST,
        preferred_element_type=jnp.float32,
    )


def stencil(padded, taps, height, width, flipped):
    total = jnp.zeros((height, width, padded.shape[2]), jnp.float32)
    for tap_row in range(3):
        for tap_col in range(3):
            if flipped:
                window = padded[
                    2 - tap_row : 2 - tap_row + height, 2 - tap_col : 2 - tap_col + width
                ]
            else:
                window = padded[tap_row : tap_row + height, tap_col : tap_col + width]
            total = total + taps[3 * tap_row + tap_col] * window.astype(jnp.float32)
    return total


def attend(carry, inputs, key_heads, value_heads):
    grad_key, grad_value = carry
    query_block, dout_block = inputs
    softmax_scale = HD ** (-0.5)
    query_heads = query_block.reshape(-1, HEADS, HD)
    dout_heads = dout_block.reshape(-1, HEADS, HD)
    scores = (
        jnp.einsum("qhd,khd->hqk", query_heads, key_heads, preferred_element_type=jnp.float32)
        * softmax_scale
    )
    expons = jnp.exp(scores)
    probabilities = expons / jnp.sum(expons, axis=-1, keepdims=True)
    weights = probabilities.astype(jnp.bfloat16)
    attended = jnp.einsum(
        "hqk,khd->qhd", weights, value_heads, preferred_element_type=jnp.float32
    ).astype(jnp.bfloat16)
    grad_probs = jnp.einsum(
        "qhd,khd->hqk", dout_heads, value_heads, preferred_element_type=jnp.float32
    )
    deltas = jnp.einsum("qhd,qhd->hq", dout_heads, attended, preferred_element_type=jnp.float32)
    grad_scores = (probabilities * (grad_probs - deltas[:, :, None]) * softmax_scale).astype(
        jnp.bfloat16
    )
    grad_query = jnp.einsum(
        "hqk,khd->qhd", grad_scores, key_heads, preferred_element_type=jnp.float32
    ).astype(jnp.bfloat16)
    grad_key = grad_key + jnp.einsum(
        "hqk,qhd->khd", grad_scores, query_heads, preferred_element_type=jnp.float32
    )
    grad_value = grad_value + jnp.einsum(
        "hqk,qhd->khd", weights, dout_heads, preferred_element_type=jnp.float32
    )
    return (
        (grad_key, grad_value),
        (attended.reshape(query_block.shape), grad_query.reshape(query_block.shape)),
    )


def on_device(image, conv_taps, w_query, w_key, w_value, w_out, grad_out):
    height, width, channels = image.shape
    padded = with_halo(image, (("row", 0), ("col", 1)), 1)
    mixed = image.astype(jnp.float32) + stencil(padded, conv_taps, height, width, False)
    hidden = mixed.astype(jnp.bfloat16)
    flat_hidden = hidden.reshape(-1, channels)
    query = jnp.dot(flat_hidden, w_query, preferred_element_type=jnp.float32).astype(jnp.bfloat16)
    pooled = (
        hidden.astype(jnp.float32)
        .reshape(height // POOL, POOL, width // POOL, POOL, channels)
        .mean(axis=(1, 3))
    )
    centre = jnp.mean(pooled, axis=-1, keepdims=True)
    spread = jnp.mean(jnp.square(pooled - centre), axis=-1, keepdims=True)
    inverse = lax.rsqrt(spread + EPSILON)
    standard = (pooled - centre) * inverse
    normed = standard.astype(jnp.bfloat16)
    gathered = lax.all_gather(normed, "col", axis=1, tiled=True)
    pooled_rows, pooled_cols = (gathered.shape[0], gathered.shape[1])
    key_cells = gathered.reshape(-1, channels)
    keys = jnp.dot(key_cells, w_key, preferred_element_type=jnp.float32).astype(jnp.bfloat16)
    values = jnp.dot(key_cells, w_value, preferred_element_type=jnp.float32).astype(jnp.bfloat16)
    flat_grad = grad_out.reshape(-1, channels)
    dout = contract_last(flat_grad, w_out).astype(jnp.bfloat16)
    total_rows = flat_hidden.shape[0]
    block_rows = math.gcd(total_rows, 512)
    blocks = total_rows // block_rows
    key_heads = keys.reshape(-1, HEADS, HD)
    value_heads = values.reshape(-1, HEADS, HD)
    empty_grad = jnp.zeros(key_heads.shape, jnp.float32)
    carry, produced = lax.scan(
        partial(attend, key_heads=key_heads, value_heads=value_heads),
        (empty_grad, empty_grad),
        (query.reshape(blocks, block_rows, channels), dout.reshape(blocks, block_rows, channels)),
    )
    grad_key = carry[0].reshape(pooled_rows, pooled_cols, channels)
    grad_value = carry[1].reshape(pooled_rows, pooled_cols, channels)
    attended = produced[0].reshape(-1, channels)
    grad_query = produced[1].reshape(-1, channels)
    grad_wout = contract_first(attended, flat_grad)
    grad_wquery = contract_first(flat_hidden, grad_query)
    grad_hidden = contract_last(grad_query, w_query)
    key_float = w_key.astype(jnp.float32)
    value_float = w_value.astype(jnp.float32)
    flat_key = grad_key.reshape(-1, channels)
    flat_value = grad_value.reshape(-1, channels)
    cell_terms = exact_last(flat_key, key_float) + exact_last(flat_value, value_float)
    cells_float = key_cells.astype(jnp.float32)
    grad_wkey = exact_first(cells_float, flat_key)
    grad_wvalue = exact_first(cells_float, flat_value)
    grad_normed = lax.psum_scatter(
        cell_terms.reshape(pooled_rows, pooled_cols, channels).astype(jnp.bfloat16),
        "col",
        scatter_dimension=1,
        tiled=True,
    ).astype(jnp.float32)
    grad_pooled = (
        grad_normed
        - jnp.mean(grad_normed, axis=-1, keepdims=True)
        - standard * jnp.mean(grad_normed * standard, axis=-1, keepdims=True)
    ) * inverse
    spread_back = jnp.broadcast_to(
        (grad_pooled / (POOL * POOL))[:, None, :, None, :],
        (height // POOL, POOL, width // POOL, POOL, channels),
    ).reshape(height, width, channels)
    grad_mixed = (
        grad_out.astype(jnp.float32) + grad_hidden.reshape(height, width, channels) + spread_back
    )
    grad_padded = with_halo(grad_mixed.astype(jnp.bfloat16), (("row", 0), ("col", 1)), 1).astype(
        grad_mixed.dtype
    )
    grad_image = (grad_mixed + stencil(grad_padded, conv_taps, height, width, True)).astype(
        jnp.bfloat16
    )
    tap_list = []
    for tap_row in range(3):
        for tap_col in range(3):
            window = padded[tap_row : tap_row + height, tap_col : tap_col + width].astype(
                jnp.float32
            )
            tap_list.append(jnp.sum(grad_mixed * window, axis=(0, 1)))
    tap_terms = jnp.stack(tap_list, axis=0)
    weight_terms = jnp.concatenate([grad_wquery, grad_wkey, grad_wvalue, grad_wout], axis=1)
    column_sums = (
        lax.psum_scatter(
            weight_terms.astype(jnp.bfloat16), "col", scatter_dimension=1, tiled=True
        ).astype(jnp.float32),
        lax.psum_scatter(
            tap_terms.astype(jnp.bfloat16), "col", scatter_dimension=1, tiled=True
        ).astype(jnp.float32),
    )
    grad_weights, grad_conv = (
        lax.psum(column_sums[0].astype(jnp.bfloat16), "row").astype(jnp.float32),
        lax.psum(column_sums[1].astype(jnp.bfloat16), "row").astype(jnp.float32),
    )
    return (grad_image, grad_weights, grad_conv)


def solution(mesh):
    return jax.shard_map(
        on_device,
        mesh=mesh,
        in_specs=(P("row", "col", None), P(), P(), P(), P(), P(), P("row", "col", None)),
        out_specs=(P("row", "col", None), P(None, "col"), P(None, "col")),
        check_vma=False,
    )
```

profile of v0, /device:TPU:0, one launch (start us, length us, event | category | flops | bytes accessed | tf_op | source)
XLA Modules:
  0.0 293.8 jit_solution(12890035376737956254)
XLA Ops:
  8.1 4.9 %collective-permute-start = (bf16[1,32,768]{2,1,0:T(8,128)(2,1)S(1)}, bf16[1,32,768]{2,1,0:T(8,128)(2,1)S(1)}, u32[]{:S(2)}, u32[]{:S(2)}) collective-permute-start(bf16[1,32,768]{2,1,0:T(8,128)(2,1)S(1)} %get-tuple-element.78), channel_id=1, source_target_pairs={{0,8},{8,16},{16,24},{1,9},{9,17},{17,25},{2,10},{10,18},{18,26},{... | collective-permute-start | bytes 147464 | tf_op jit(solution)/shard_map/ppermute | solution.py:22
  14.3 2.4 convolution_convert_fusion.4
  16.8 2.2 collective-permute-done.1
  21.2 3.7 %collective-permute-start.2 = (bf16[18,1,768]{2,1,0:T(2,128)(2,1)}, bf16[18,1,768]{2,1,0:T(2,128)(2,1)}, u32[]{:S(2)}, u32[]{:S(2)}) collective-permute-start(bf16[18,1,768]{2,1,0:T(2,128)(2,1)} %get-tuple-element.75), channel_id=1, source_target_pairs={{0,1},{1,2},{2,3},{3,4},{4,5},{5,6},{6,7},{8,9},{9,10},{10,11},{11... | collective-permute-start | bytes 82952 | tf_op jit(solution)/shard_map/ppermute | solution.py:22
  27.7 5.4 %fusion.28 = bf16[16,32,768]{2,1,0:T(8,128)(2,1)S(1)} fusion(bf16[16,32,768]{2,1,0:T(8,128)(2,1)S(1)} %copy-done.5, bf16[1,32,768]{2,1,0:T(8,128)(2,1)} %copy-done.23, bf16[1,32,768]{2,1,0:T(8,128)(2,1)} %copy-done.22, f32[768]{0:T(1024)} %get-tuple-element.69, f32[768]{0:T(1024)} %get-tuple-element.70, f32[768]{0:T(1024)S(1)} %get-tuple-element.63, ...), kind=kLoop, calls=%fused_computation.62 | loop fusion | flops 20447232 | bytes 2638848 | tf_op jit(solution)/shard_map/convert_element_type | solution.py:119
  35.7 2.4 copy.51
  40.3 14.0 %all_gather.3 = bf16[2,32,768]{2,0,1:T(2,128)(2,1)S(1)} all-gather(bf16[2,4,768]{2,0,1:T(2,128)(2,1)S(1)} %copy.49), channel_id=1, replica_groups=mesh['row'=4,'col'=8] {'col'}, dimensions={1}, use_global_device_ids=true | all-gather | bytes 110592 | tf_op jit(solution)/shard_map/all_gather | solution.py:132
  59.7 2.6 fusion.63
  64.6 3.3 %fusion.32 = f32[12,64,64]{2,1,0:T(8,128)} fusion(bf16[512,12,64]{0,2,1:T(8,128)(2,1)} %bitcast.91, f32[12,512,64]{1,2,0:T(8,128)S(1)} %fusion.42, f32[12,512,64]{1,2,0:T(8,128)} %fusion.63, bf16[12,512,64]{1,2,0:T(8,128)(2,1)S(1)} %bitcast.81, bf16[12,64,512]{2,1,0:T(8,128)(2,1)} %convolution_convert_fusion.7), kind=kOutput, calls=%fused_computation.86 | convolution fusion | flops 53090368 | bytes 5701632 | tf_op jit(solution)/shard_map/while/body/eval_jaxpr/hqk,qhd->khd/dot_general | solution.py:103
  67.9 3.3 %convolution_convert_fusion.6 = bf16[12,64,512]{2,1,0:T(8,128)(2,1)} fusion(bf16[64,12,64]{0,2,1:T(8,128)(2,1)} %bitcast.103, f32[12,512,64]{1,2,0:T(8,128)S(1)} %fusion.42, f32[12,512,64]{1,2,0:T(8,128)} %fusion.63, bf16[12,512,64]{1,2,0:T(8,128)(2,1)S(1)} %bitcast.82, bf16[12,64,512]{2,1,0:T(8,128)(2,1)} %convolution_convert_fusion.7), kind=kOutput, calls=%fused_computation.74 | convolution fusion | flops 53483584 | bytes 5603328 | tf_op jit(solution)/shard_map/while/body/eval_jaxpr/hqk,khd->qhd/dot_general | solution.py:100
  71.2 2.8 fusion.62
  84.1 2.9 copy.57
  89.1 42.7 %all-reduce.6.cloned.1.call-done = bf16[2,32,768]{2,1,0:T(8,128)(2,1)} async-done(((bf16[2,32,768]{2,1,0:T(8,128)(2,1)}), bf16[2,32,768]{2,1,0:T(8,128)(2,1)}) %all-reduce.6.cloned.1.call-update) | async-done | bytes 98320
  133.8 6.3 %fusion.16 = (bf16[768]{0:T(1024)(128)(2,1)S(1)}, bf16[768]{0:T(1024)(128)(2,1)S(1)}, bf16[768]{0:T(1024)(128)(2,1)S(1)}, bf16[768]{0:T(1024)(128)(2,1)S(1)}, bf...) fusion(bf16[18,1,768]{2,1,0:T(2,128)(2,1)} %collective-permute-, ...), kind=kOutput, calls=%fused_computation.36 | convolution fusion | flops 625599744 | bytes 8523264 | tf_op jit(solution)/shard_map/dot_general | solution.py:38
  145.4 2.6 stack.49
  149.7 4.3 %pad_maximum_fusion = bf16[768,3072]{0,1:T(8,128)(2,1)} fusion(bf16[768,768]{0,1:T(8,128)(2,1)} %convolution_convert_fusion.1, bf16[768,768]{0,1:T(8,128)(2,1)S(1)} %copy-done.1, bf16[768,768]{0,1:T(8,128)(2,1)S(1)} %copy-done.2, bf16[768,768]{0,1:T(8,128)(2,1)} %convolution_convert_fusion), kind=kLoop, calls=%fused_computation.1 | loop fusion | flops 18874368 | bytes 9437184 | tf_op jit(solution)/shard_map/concatenate | solution.py:197
  156.5 4.5 %collective-permute-start.4 = (bf16[1,32,768]{2,1,0:T(8,128)(2,1)S(1)}, bf16[1,32,768]{2,1,0:T(8,128)(2,1)S(1)}, u32[]{:S(2)}, u32[]{:S(2)}) collective-permute-start(bf16[1,32,768]{2,1,0:T(8,128)(2,1)S(1)} %get-tuple-element.76), channel_id=1, source_target_pairs={{0,8},{8,16},{16,24},{1,9},{9,17},{17,25},{2,10},{10,18},{18,26},{... | collective-permute-start | bytes 147464 | tf_op jit(solution)/shard_map/ppermute | solution.py:22
  164.2 3.0 %collective-permute-start.6 = (bf16[18,1,768]{2,1,0:T(2,128)(2,1)S(1)}, bf16[18,1,768]{2,1,0:T(2,128)(2,1)S(1)}, u32[]{:S(2)}, u32[]{:S(2)}) collective-permute-start(bf16[18,1,768]{2,1,0:T(2,128)(2,1)S(1)} %get-tuple-element.72), channel_id=1, source_target_pairs={{0,1},{1,2},{2,3},{3,4},{4,5},{5,6},{6,7},{8,9},{9,10},{10,11},{11... | collective-permute-start | bytes 82952 | tf_op jit(solution)/shard_map/ppermute | solution.py:22
  167.2 15.0 %reduce-scatter.8.cloned.1.call-done = bf16[96,9]{1,0:T(8,128)(2,1)} async-done(((bf16[768,9]{1,0:T(8,128)(2,1)}), bf16[96,9]{1,0:T(8,128)(2,1)}) %reduce-scatter.8.cloned.1.call-update) | async-done | bytes 1744
  183.0 9.8 %psum.15 = bf16[9,96]{1,0:T(8,128)(2,1)S(1)} all-reduce(bf16[9,96]{1,0:T(8,128)(2,1)S(1)} %copy.70), channel_id=1, replica_groups=mesh['row'=4,'col'=8] {'row'}, use_global_device_ids=true, to_apply=%region_19.20 | all-reduce | flops 864 | bytes 3456 | tf_op jit(solution)/shard_map/psum | solution.py:208
  193.4 44.2 %reduce-scatter.6.cloned.1.call-done = bf16[768,384]{0,1:T(8,128)(2,1)} async-done(((bf16[768,3072]{0,1:T(8,128)(2,1)}), bf16[768,384]{0,1:T(8,128)(2,1)}) %reduce-scatter.6.cloned.1.call-update) | async-done | bytes 589840 | tf_op jit(solution)/shard_map/reduce_scatter | solution.py:199
  239.1 2.6 fusion.20
  241.6 43.3 %all-reduce.4.cloned.1.call-done = bf16[768,384]{0,1:T(8,128)(2,1)} async-done(((bf16[768,384]{0,1:T(8,128)(2,1)}), bf16[768,384]{0,1:T(8,128)(2,1)}) %all-reduce.4.cloned.1.call-update) | async-done | bytes 589840 | tf_op jit(solution)/shard_map/psum | solution.py:207
  285.0 2.3 copy.58
  (138 shorter events, 48.4 us)
Async XLA Ops:
  7.2 26.9 %copy-start = (bf16[768,768]{1,0:T(8,128)(2,1)S(1)}, bf16[768,768]{1,0:T(8,128)(2,1)}, u32[]{:S(2)}) copy-start(bf16[768,768]{1,0:T(8,128)(2,1)} %param.9) | copy-start | bytes 3538948
  7.2 124.6 %all-reduce.6.cloned.1.call-start = ((), (), s32[]{:S(2)}) async-start(), calls=%async_computation.5 | async-start | bytes 196608
  8.1 8.6 %collective-permute-start = (bf16[1,32,768]{2,1,0:T(8,128)(2,1)S(1)}, bf16[1,32,768]{2,1,0:T(8,128)(2,1)S(1)}, u32[]{:S(2)}, u32[]{:S(2)}) collective-permute-start(bf16[1,32,768]{2,1,0:T(8,128)(2,1)S(1)} %get-tuple-element.78), channel_id=1, source_target_pairs={{0,8},{8,16},{16,24},{1,9},{9,17},{17,25},{2,10},{10,18},{18,26},{... | collective-permute-start | bytes 147464 | tf_op jit(solution)/shard_map/ppermute | solution.py:22
  13.0 6.0 %collective-permute-start.1 = (bf16[1,32,768]{2,1,0:T(8,128)(2,1)S(1)}, bf16[1,32,768]{2,1,0:T(8,128)(2,1)S(1)}, u32[]{:S(2)}, u32[]{:S(2)}) collective-permute-start(bf16[1,32,768]{2,1,0:T(8,128)(2,1)S(1)} %get-tuple-element.79), channel_id=1, source_target_pairs={{8,0},{16,8},{24,16},{9,1},{17,9},{25,17},{10,2},{18,10},{26,18},{... | collective-permute-start | bytes 147464 | tf_op jit(solution)/shard_map/ppermute | solution.py:24
  16.7 8.1 %copy-start.33 = (f32[9,768]{1,0:T(8,128)S(1)}, f32[9,768]{1,0:T(8,128)}, u32[]{:S(2)}) copy-start(f32[9,768]{1,0:T(8,128)} %param.8) | copy-start | bytes 82948
  16.7 8.8 %copy-start.22 = (bf16[1,32,768]{2,1,0:T(8,128)(2,1)}, bf16[1,32,768]{2,1,0:T(8,128)(2,1)S(1)}, u32[]{:S(2)}) copy-start(bf16[1,32,768]{2,1,0:T(8,128)(2,1)S(1)} %collective-permute-done) | copy-start | bytes 147460
  19.0 6.5 %copy-start.23 = (bf16[1,32,768]{2,1,0:T(8,128)(2,1)}, bf16[1,32,768]{2,1,0:T(8,128)(2,1)S(1)}, u32[]{:S(2)}) copy-start(bf16[1,32,768]{2,1,0:T(8,128)(2,1)S(1)} %collective-permute-done.1) | copy-start | bytes 147460
  19.0 6.5 %copy-start.17 = (bf16[18,32,768]{2,1,0:T(8,128)(2,1)}, bf16[18,32,768]{2,1,0:T(8,128)(2,1)S(1)}, u32[]{:S(2)}) copy-start(bf16[18,32,768]{2,1,0:T(8,128)(2,1)S(1)} %constant_dynamic-update-slice_fusion) | copy-start | bytes 2654212
  19.9 7.8 %collective-permute-start.3 = (bf16[18,1,768]{2,1,0:T(2,128)(2,1)}, bf16[18,1,768]{2,1,0:T(2,128)(2,1)}, u32[]{:S(2)}, u32[]{:S(2)}) collective-permute-start(bf16[18,1,768]{2,1,0:T(2,128)(2,1)} %get-tuple-element.74), channel_id=1, source_target_pairs={{1,0},{2,1},{3,2},{4,3},{5,4},{6,5},{7,6},{9,8},{10,9},{11,10},{12... | collective-permute-start | bytes 82952 | tf_op jit(solution)/shard_map/ppermute | solution.py:24
  21.2 6.5 %collective-permute-start.2 = (bf16[18,1,768]{2,1,0:T(2,128)(2,1)}, bf16[18,1,768]{2,1,0:T(2,128)(2,1)}, u32[]{:S(2)}, u32[]{:S(2)}) collective-permute-start(bf16[18,1,768]{2,1,0:T(2,128)(2,1)} %get-tuple-element.75), channel_id=1, source_target_pairs={{0,1},{1,2},{2,3},{3,4},{4,5},{5,6},{6,7},{8,9},{9,10},{10,11},{11... | collective-permute-start | bytes 82952 | tf_op jit(solution)/shard_map/ppermute | solution.py:22
  35.7 18.5 %copy-start.3 = (bf16[768,768]{1,0:T(8,128)(2,1)S(1)}, bf16[768,768]{1,0:T(8,128)(2,1)}, u32[]{:S(2)}) copy-start(bf16[768,768]{1,0:T(8,128)(2,1)} %param.10) | copy-start | bytes 3538948
  71.2 4.9 %copy-start.4 = (bf16[768,768]{1,0:T(8,128)(2,1)S(1)}, bf16[768,768]{1,0:T(8,128)(2,1)}, u32[]{:S(2)}) copy-start(bf16[768,768]{1,0:T(8,128)(2,1)} %param.11) | copy-start | bytes 3538948
  78.0 104.2 %reduce-scatter.8.cloned.1.call-start = ((), (), s32[]{:S(2)}) async-start(), calls=%async_computation.4 | async-start | bytes 221184
  87.0 44.7 %copy-start.21 = (f32[2,4,768]{2,1,0:T(4,128)S(1)}, f32[2,4,768]{2,1,0:T(4,128)}, u32[]{:S(2)}) copy-start(f32[2,4,768]{2,1,0:T(4,128)} %copy-done.20) | copy-start | bytes 73732
  87.0 44.7 %copy-start.30 = (f32[2,4]{1,0:T(2,128)S(1)}, f32[2,4]{1,0:T(2,128)}, u32[]{:S(2)}) copy-start(f32[2,4]{1,0:T(2,128)} %copy-done.29) | copy-start | bytes 100
  87.1 44.7 %copy-start.32 = (f32[2,4]{1,0:T(2,128)S(1)}, f32[2,4]{1,0:T(2,128)}, u32[]{:S(2)}) copy-start(f32[2,4]{1,0:T(2,128)} %copy-done.31) | copy-start | bytes 100
  133.8 15.9 %copy-start.1 = (bf16[768,768]{0,1:T(8,128)(2,1)S(1)}, bf16[768,768]{0,1:T(8,128)(2,1)}, u32[]{:S(2)}) copy-start(bf16[768,768]{0,1:T(8,128)(2,1)} %convolution_convert_fusion.2) | copy-start | bytes 3538948
  133.8 15.9 %copy-start.2 = (bf16[768,768]{0,1:T(8,128)(2,1)S(1)}, bf16[768,768]{0,1:T(8,128)(2,1)}, u32[]{:S(2)}) copy-start(bf16[768,768]{0,1:T(8,128)(2,1)} %convolution_convert_fusion.3) | copy-start | bytes 3538948
  149.7 87.9 %reduce-scatter.6.cloned.1.call-start = ((), (), s32[]{:S(2)}) async-start(), calls=%async_computation.2 | async-start | bytes 5308416 | tf_op jit(solution)/shard_map/reduce_scatter | solution.py:199
  154.1 130.9 %all-reduce.4.cloned.1.call-start = ((), (), s32[]{:S(2)}) async-start(), calls=%async_computation.3 | async-start | bytes 1179648 | tf_op jit(solution)/shard_map/psum | solution.py:207
  155.2 6.0 %collective-permute-start.5 = (bf16[1,32,768]{2,1,0:T(8,128)(2,1)S(1)}, bf16[1,32,768]{2,1,0:T(8,128)(2,1)S(1)}, u32[]{:S(2)}, u32[]{:S(2)}) collective-permute-start(bf16[1,32,768]{2,1,0:T(8,128)(2,1)S(1)} %get-tuple-element.77), channel_id=1, source_target_pairs={{8,0},{16,8},{24,16},{9,1},{17,9},{25,17},{10,2},{18,10},{26,18},{... | collective-permute-start | bytes 147464 | tf_op jit(solution)/shard_map/ppermute | solution.py:24
  156.5 6.3 %collective-permute-start.4 = (bf16[1,32,768]{2,1,0:T(8,128)(2,1)S(1)}, bf16[1,32,768]{2,1,0:T(8,128)(2,1)S(1)}, u32[]{:S(2)}, u32[]{:S(2)}) collective-permute-start(bf16[1,32,768]{2,1,0:T(8,128)(2,1)S(1)} %get-tuple-element.76), channel_id=1, source_target_pairs={{0,8},{8,16},{16,24},{1,9},{9,17},{17,25},{2,10},{10,18},{18,26},{... | collective-permute-start | bytes 147464 | tf_op jit(solution)/shard_map/ppermute | solution.py:22
  162.9 74.8 %collective-permute-start.7 = (bf16[18,1,768]{2,1,0:T(2,128)(2,1)S(1)}, bf16[18,1,768]{2,1,0:T(2,128)(2,1)S(1)}, u32[]{:S(2)}, u32[]{:S(2)}) collective-permute-start(bf16[18,1,768]{2,1,0:T(2,128)(2,1)S(1)} %get-tuple-element.73), channel_id=1, source_target_pairs={{1,0},{2,1},{3,2},{4,3},{5,4},{6,5},{7,6},{9,8},{10,9},{11,10},{12... | collective-permute-start | bytes 82952 | tf_op jit(solution)/shard_map/ppermute | solution.py:24
  164.2 73.5 %collective-permute-start.6 = (bf16[18,1,768]{2,1,0:T(2,128)(2,1)S(1)}, bf16[18,1,768]{2,1,0:T(2,128)(2,1)S(1)}, u32[]{:S(2)}, u32[]{:S(2)}) collective-permute-start(bf16[18,1,768]{2,1,0:T(2,128)(2,1)S(1)} %get-tuple-element.72), channel_id=1, source_target_pairs={{0,1},{1,2},{2,3},{3,4},{4,5},{5,6},{6,7},{8,9},{9,10},{10,11},{11... | collective-permute-start | bytes 82952 | tf_op jit(solution)/shard_map/ppermute | solution.py:22
  (23 other events, 44.4 us)
Sparse Core Ops, SparseCore 0:
  78.2 53.5 all-reduce.5
  149.8 32.3 reduce-scatter.7
  184.5 53.0 reduce-scatter.5
  240.5 44.4 all-reduce.3
where the time goes:
time: 295 us; the launch traced here: 294 us
  waiting for transfers between devices  149 us (51%)
  matrix products  38.1 us (13%)
  local copies, waits for them, and re-layouts  29.3 us (10%)
  blocking collectives  23.8 us (8%)
  starting transfers between devices  21.6 us (7%)
  other arithmetic  16.9 us (6%)
  between operations  14.9 us (5%)
    unnamed x6, waiting for transfers between devices  57.7 us
    reduce_scatter x1, waiting for transfers between devices, on_device(): lax.psum_scatter(weight_terms.astype(jnp.bfloat16), 'col', scatter_dimens...  44.2 us
    psum x1, waiting for transfers between devices, on_device(): lax.psum(column_sums[0].astype(jnp.bfloat16), 'row').astype(jnp.float32)  43.3 us
    ppermute x4, starting transfers between devices, with_halo(): lax.ppermute(tail, axis, [(i, (i + 1) % count) for i in range(ends)])  16.1 us
    all_gather x1, blocking collectives, on_device(): gathered = lax.all_gather(normed, 'col', axis=1, tiled=True)  14 us
    psum x1, blocking collectives, on_device(): lax.psum(column_sums[1].astype(jnp.bfloat16), 'row').astype(jnp.float32)  9.8 us
    unnamed x76, local copies, waits for them, and re-layouts  9.51 us
    dot_general x2, matrix products, contract_last(): lax.dot_general(left, right, (((1,), (1,)), ((), ())), preferred_element_...  8.7 us
  transfers between devices with their start and end apart: 12, of which 7 were waited for; matrix products, arithmetic and copies ran while one was open for 8% of the time, Pallas kernels for 0%

commit v1 on v0

--- a/solution.py
+++ b/solution.py
@@ -9,6 +9,11 @@
 HD = 64
 POOL = 8
 EPSILON = 1e-05
+
+
+def choose_the_panel(base_x, axis_tag):
+    o_now = jnp.sum(lax.all_gather(base_x, axis_name=axis_tag), axis=0)
+    return o_now
 
 
 def with_halo(cells, sides, width):
@@ -204,7 +209,7 @@
         ).astype(jnp.float32),
     )
     grad_weights, grad_conv = (
-        lax.psum(column_sums[0].astype(jnp.bfloat16), "row").astype(jnp.float32),
+        choose_the_panel(column_sums[0].astype(jnp.bfloat16), "row").astype(jnp.float32),
         lax.psum(column_sums[1].astype(jnp.bfloat16), "row").astype(jnp.float32),
     )
     return (grad_image, grad_weights, grad_conv)

time: 295 us -> 278 us (0.942)
  waiting for transfers between devices: 149 us -> 136 us
  local copies, waits for them, and re-layouts: 29.3 us -> 24 us
    psum x1 -> x0, waiting for transfers between devices: 43.3 us -> none  [on_device(): lax.psum(column_sums[0].astype(jnp.bfloat16), 'row').astype(jnp.float32)]
    all_gather x0 -> x1, waiting for transfers between devices: none -> 21.9 us  [choose_the_panel(): o_now = jnp.sum(lax.all_gather(base_x, axis_name=axis_tag), axis=0)]
    another operation x10, local copies, waits for them, and re-layouts: 7.91 us -> 0.12 us  [on_device(): tap_terms = jnp.stack(tap_list, axis=0)]
    reduce_scatter x1, waiting for transfers between devices: 44.2 us -> 49.6 us  [on_device(): lax.psum_scatter(weight_terms.astype(jnp.bfloat16), 'col', scatter_dimens...]
    all_gather x0 -> x1, local copies, waits for them, and re-layouts: none -> 4.52 us  [choose_the_panel(): o_now = jnp.sum(lax.all_gather(base_x, axis_name=axis_tag), axis=0)]
    reduce_sum x0 -> x1, other arithmetic: none -> 4 us  [choose_the_panel(): o_now = jnp.sum(lax.all_gather(base_x, axis_name=axis_tag), axis=0)]
    unnamed x6, waiting for transfers between devices: 57.7 us -> 61.1 us
    unnamed x76 -> x72, local copies, waits for them, and re-layouts: 9.51 us -> 7.43 us
  transfers between devices with their start and end apart: 12 -> 12, of which waited for: 7 -> 7; matrix products, arithmetic and copies ran while one was open for 8% -> 10% of each run, Pallas kernels for 0% -> 0%
where the time goes in v1:
time: 278 us; the launch traced here: 277 us
  waiting for transfers between devices  136 us (49%)
  matrix products  35.2 us (13%)
  blocking collectives  26 us (9%)
  local copies, waits for them, and re-layouts  24 us (9%)
  starting transfers between devices  21.6 us (8%)
  other arithmetic  18.7 us (7%)
  between operations  15 us (5%)
    unnamed x6, waiting for transfers between devices  61.1 us
    reduce_scatter x1, waiting for transfers between devices, on_device(): lax.psum_scatter(weight_terms.astype(jnp.bfloat16), 'col', scatter_dimens...  49.6 us
    all_gather x1, waiting for transfers between devices, choose_the_panel(): o_now = jnp.sum(lax.all_gather(base_x, axis_name=axis_tag), axis=0)  21.9 us
    ppermute x4, starting transfers between devices, with_halo(): lax.ppermute(tail, axis, [(i, (i + 1) % count) for i in range(ends)])  16.1 us
    all_gather x1, blocking collectives, on_device(): gathered = lax.all_gather(normed, 'col', axis=1, tiled=True)  16.1 us
    psum x1, blocking collectives, on_device(): lax.psum(column_sums[1].astype(jnp.bfloat16), 'row').astype(jnp.float32)  9.92 us
    dot_general x2, matrix products, contract_last(): lax.dot_general(left, right, (((1,), (1,)), ((), ())), preferred_element_...  8.45 us
    unnamed x72, local copies, waits for them, and re-layouts  7.43 us
  transfers between devices with their start and end apart: 12, of which 7 were waited for; matrix products, arithmetic and copies ran while one was open for 10% of the time, Pallas kernels for 0%

profile of v1, /device:TPU:0, one launch (start us, length us, event | category | flops | bytes accessed | tf_op | source)
XLA Modules:
  0.0 277.1 jit_solution(15146009227457146195)
XLA Ops:
  8.1 4.9 %collective-permute-start = (bf16[1,32,768]{2,1,0:T(8,128)(2,1)S(1)}, bf16[1,32,768]{2,1,0:T(8,128)(2,1)S(1)}, u32[]{:S(2)}, u32[]{:S(2)}) collective-permute-start(bf16[1,32,768]{2,1,0:T(8,128)(2,1)S(1)} %get-tuple-element.72), channel_id=1, source_target_pairs={{0,8},{8,16},{16,24},{1,9},{9,17},{17,25},{2,10},{10,18},{18,26},{... | collective-permute-start | bytes 147464 | tf_op jit(solution)/shard_map/ppermute | solution.py:27
  14.3 2.4 convolution_convert_fusion.4
  21.2 3.6 %collective-permute-start.2 = (bf16[18,1,768]{2,1,0:T(2,128)(2,1)}, bf16[18,1,768]{2,1,0:T(2,128)(2,1)}, u32[]{:S(2)}, u32[]{:S(2)}) collective-permute-start(bf16[18,1,768]{2,1,0:T(2,128)(2,1)} %get-tuple-element.69), channel_id=1, source_target_pairs={{0,1},{1,2},{2,3},{3,4},{4,5},{5,6},{6,7},{8,9},{9,10},{10,11},{11... | collective-permute-start | bytes 82952 | tf_op jit(solution)/shard_map/ppermute | solution.py:27
  25.9 5.1 %fusion.28 = bf16[16,32,768]{2,1,0:T(8,128)(2,1)S(1)} fusion(bf16[16,32,768]{2,1,0:T(8,128)(2,1)S(1)} %copy-done.3, bf16[1,32,768]{2,1,0:T(8,128)(2,1)} %copy-done.20, bf16[1,32,768]{2,1,0:T(8,128)(2,1)} %copy-done.18, f32[768]{0:T(1024)} %get-tuple-element.63, f32[768]{0:T(1024)} %get-tuple-element.64, f32[768]{0:T(1024)S(1)} %get-tuple-element.57, ...), kind=kLoop, calls=%fused_computation.62 | loop fusion | flops 20447232 | bytes 2638848 | tf_op jit(solution)/shard_map/convert_element_type | solution.py:124
  33.5 2.4 copy.49
  38.1 16.1 %all_gather.9 = bf16[2,32,768]{2,0,1:T(2,128)(2,1)S(1)} all-gather(bf16[2,4,768]{2,0,1:T(2,128)(2,1)S(1)} %copy.47), channel_id=1, replica_groups=mesh['row'=4,'col'=8] {'col'}, dimensions={1}, use_global_device_ids=true | all-gather | bytes 110592 | tf_op jit(solution)/shard_map/all_gather | solution.py:137
  59.6 2.6 fusion.63
  64.5 3.3 %fusion.32 = f32[12,64,64]{2,1,0:T(8,128)} fusion(bf16[512,12,64]{0,2,1:T(8,128)(2,1)} %bitcast.93, f32[12,512,64]{1,2,0:T(8,128)S(1)} %fusion.42, f32[12,512,64]{1,2,0:T(8,128)} %fusion.63, bf16[12,512,64]{1,2,0:T(8,128)(2,1)S(1)} %bitcast.83, bf16[12,64,512]{2,1,0:T(8,128)(2,1)} %convolution_convert_fusion.7), kind=kOutput, calls=%fused_computation.86 | convolution fusion | flops 53090368 | bytes 5701632 | tf_op jit(solution)/shard_map/while/body/eval_jaxpr/hqk,qhd->khd/dot_general | solution.py:108
  67.8 3.3 %convolution_convert_fusion.6 = bf16[12,64,512]{2,1,0:T(8,128)(2,1)} fusion(bf16[64,12,64]{0,2,1:T(8,128)(2,1)} %bitcast.105, f32[12,512,64]{1,2,0:T(8,128)S(1)} %fusion.42, f32[12,512,64]{1,2,0:T(8,128)} %fusion.63, bf16[12,512,64]{1,2,0:T(8,128)(2,1)S(1)} %bitcast.84, bf16[12,64,512]{2,1,0:T(8,128)(2,1)} %convolution_convert_fusion.7), kind=kOutput, calls=%fused_computation.74 | convolution fusion | flops 53483584 | bytes 5603328 | tf_op jit(solution)/shard_map/while/body/eval_jaxpr/hqk,khd->qhd/dot_general | solution.py:105
  71.1 2.7 fusion.62
  81.1 2.5 pad_maximum_fusion
  85.6 2.9 %copy.55 = bf16[512,12,64]{2,1,0:T(8,128)(2,1)S(1)} copy(bf16[512,12,64]{0,2,1:T(8,128)(2,1)} %bitcast.94) | data formatting | bytes 1572864 | tf_op jit(solution)/shard_map/while/body/eval_jaxpr/convert_element_type | solution.py:107
  90.6 41.0 %all-reduce.3.cloned.1.call-done = bf16[2,32,768]{2,1,0:T(8,128)(2,1)} async-done(((bf16[2,32,768]{2,1,0:T(8,128)(2,1)}), bf16[2,32,768]{2,1,0:T(8,128)(2,1)}) %all-reduce.3.cloned.1.call-update) | async-done | bytes 98320
  133.6 6.1 %fusion.16 = (bf16[768]{0:T(1024)(128)(2,1)S(1)}, bf16[768]{0:T(1024)(128)(2,1)S(1)}, bf16[768]{0:T(1024)(128)(2,1)S(1)}, bf16[768]{0:T(1024)(128)(2,1)S(1)}, bf...) fusion(bf16[18,1,768]{2,1,0:T(2,128)(2,1)} %collective-permute-, ...), kind=kOutput, calls=%fused_computation.36 | convolution fusion | flops 625599744 | bytes 8523264 | tf_op jit(solution)/shard_map/dot_general | solution.py:43
  140.7 49.6 %reduce-scatter.6.cloned.1.call-done = bf16[768,384]{0,1:T(8,128)(2,1)} async-done(((bf16[768,3072]{0,1:T(8,128)(2,1)}), bf16[768,384]{0,1:T(8,128)(2,1)}) %reduce-scatter.6.cloned.1.call-update) | async-done | bytes 589840 | tf_op jit(solution)/shard_map/reduce_scatter | solution.py:204
  191.7 4.5 %collective-permute-start.4 = (bf16[1,32,768]{2,1,0:T(8,128)(2,1)S(1)}, bf16[1,32,768]{2,1,0:T(8,128)(2,1)S(1)}, u32[]{:S(2)}, u32[]{:S(2)}) collective-permute-start(bf16[1,32,768]{2,1,0:T(8,128)(2,1)S(1)} %get-tuple-element.70), channel_id=1, source_target_pairs={{0,8},{8,16},{16,24},{1,9},{9,17},{17,25},{2,10},{10,18},{18,26},{... | collective-permute-start | bytes 147464 | tf_op jit(solution)/shard_map/ppermute | solution.py:27
  199.4 3.0 %collective-permute-start.6 = (bf16[18,1,768]{2,1,0:T(2,128)(2,1)S(1)}, bf16[18,1,768]{2,1,0:T(2,128)(2,1)S(1)}, u32[]{:S(2)}, u32[]{:S(2)}) collective-permute-start(bf16[18,1,768]{2,1,0:T(2,128)(2,1)S(1)} %get-tuple-element.66), channel_id=1, source_target_pairs={{0,1},{1,2},{2,3},{3,4},{4,5},{5,6},{6,7},{8,9},{9,10},{10,11},{11... | collective-permute-start | bytes 82952 | tf_op jit(solution)/shard_map/ppermute | solution.py:27
  202.4 20.1 %reduce-scatter.8.cloned.1.call-done = bf16[96,9]{1,0:T(8,128)(2,1)} async-done(((bf16[768,9]{1,0:T(8,128)(2,1)}), bf16[96,9]{1,0:T(8,128)(2,1)}) %reduce-scatter.8.cloned.1.call-update) | async-done | bytes 1744
  223.3 9.9 %psum.7 = bf16[9,96]{1,0:T(8,128)(2,1)S(1)} all-reduce(bf16[9,96]{1,0:T(8,128)(2,1)S(1)} %copy.68), channel_id=1, replica_groups=mesh['row'=4,'col'=8] {'row'}, use_global_device_ids=true, to_apply=%region_19.20 | all-reduce | flops 864 | bytes 3456 | tf_op jit(solution)/shard_map/psum | solution.py:213
  235.2 2.6 fusion.20
  237.8 21.9 %all-gather.3.cloned.1.call-done = bf16[3072,384]{0,1:T(8,128)(2,1)} async-done(((bf16[768,384]{0,1:T(8,128)(2,1)}), bf16[3072,384]{0,1:T(8,128)(2,1)}) %all-gather.3.cloned.1.call-update) | async-done | bytes 2359312 | tf_op jit(solution)/shard_map/all_gather | solution.py:15
  259.7 4.5 %reshape.111 = bf16[4,768,384]{1,0,2:T(4,128)(2,1)S(1)} reshape(bf16[3072,384]{0,1:T(8,128)(2,1)} %all-gather.3.cloned.1.call-done) | data formatting | bytes 4718592 | tf_op jit(solution)/shard_map/all_gather | solution.py:15
  264.2 4.0 %reduce_sum.154 = bf16[768,384]{0,1:T(8,128)(2,1)} reduce(bf16[4,768,384]{1,0,2:T(4,128)(2,1)S(1)} %reshape.111, bf16[]{:T(256)} %constant.33.clone.1), dimensions={0}, to_apply=%region_8.9 | reduce | flops 884736 | bytes 2949122 | tf_op jit(solution)/shard_map/reduce_sum | solution.py:15
  268.2 2.3 copy.56
  (136 shorter events, 40.7 us)
Async XLA Ops:
  7.2 24.7 %copy-start = (bf16[768,768]{1,0:T(8,128)(2,1)S(1)}, bf16[768,768]{1,0:T(8,128)(2,1)}, u32[]{:S(2)}) copy-start(bf16[768,768]{1,0:T(8,128)(2,1)} %param.9) | copy-start | bytes 3538948
  7.2 124.4 %all-reduce.3.cloned.1.call-start = ((), (), s32[]{:S(2)}) async-start(), calls=%async_computation.5 | async-start | bytes 196608
  8.1 8.6 %collective-permute-start = (bf16[1,32,768]{2,1,0:T(8,128)(2,1)S(1)}, bf16[1,32,768]{2,1,0:T(8,128)(2,1)S(1)}, u32[]{:S(2)}, u32[]{:S(2)}) collective-permute-start(bf16[1,32,768]{2,1,0:T(8,128)(2,1)S(1)} %get-tuple-element.72), channel_id=1, source_target_pairs={{0,8},{8,16},{16,24},{1,9},{9,17},{17,25},{2,10},{10,18},{18,26},{... | collective-permute-start | bytes 147464 | tf_op jit(solution)/shard_map/ppermute | solution.py:27
  13.0 6.0 %collective-permute-start.1 = (bf16[1,32,768]{2,1,0:T(8,128)(2,1)S(1)}, bf16[1,32,768]{2,1,0:T(8,128)(2,1)S(1)}, u32[]{:S(2)}, u32[]{:S(2)}) collective-permute-start(bf16[1,32,768]{2,1,0:T(8,128)(2,1)S(1)} %get-tuple-element.73), channel_id=1, source_target_pairs={{8,0},{16,8},{24,16},{9,1},{17,9},{25,17},{10,2},{18,10},{26,18},{... | collective-permute-start | bytes 147464 | tf_op jit(solution)/shard_map/ppermute | solution.py:29
  16.7 8.2 %copy-start.31 = (f32[9,768]{1,0:T(8,128)S(1)}, f32[9,768]{1,0:T(8,128)}, u32[]{:S(2)}) copy-start(f32[9,768]{1,0:T(8,128)} %param.8) | copy-start | bytes 82948
  16.7 8.1 %copy-start.18 = (bf16[1,32,768]{2,1,0:T(8,128)(2,1)}, bf16[1,32,768]{2,1,0:T(8,128)(2,1)S(1)}, u32[]{:S(2)}) copy-start(bf16[1,32,768]{2,1,0:T(8,128)(2,1)S(1)} %collective-permute-done) | copy-start | bytes 147460
  19.0 5.9 %copy-start.20 = (bf16[1,32,768]{2,1,0:T(8,128)(2,1)}, bf16[1,32,768]{2,1,0:T(8,128)(2,1)S(1)}, u32[]{:S(2)}) copy-start(bf16[1,32,768]{2,1,0:T(8,128)(2,1)S(1)} %collective-permute-done.1) | copy-start | bytes 147460
  19.0 5.9 %copy-start.14 = (bf16[18,32,768]{2,1,0:T(8,128)(2,1)}, bf16[18,32,768]{2,1,0:T(8,128)(2,1)S(1)}, u32[]{:S(2)}) copy-start(bf16[18,32,768]{2,1,0:T(8,128)(2,1)S(1)} %constant_dynamic-update-slice_fusion) | copy-start | bytes 2654212
  19.9 5.9 %collective-permute-start.3 = (bf16[18,1,768]{2,1,0:T(2,128)(2,1)}, bf16[18,1,768]{2,1,0:T(2,128)(2,1)}, u32[]{:S(2)}, u32[]{:S(2)}) collective-permute-start(bf16[18,1,768]{2,1,0:T(2,128)(2,1)} %get-tuple-element.68), channel_id=1, source_target_pairs={{1,0},{2,1},{3,2},{4,3},{5,4},{6,5},{7,6},{9,8},{10,9},{11,10},{12... | collective-permute-start | bytes 82952 | tf_op jit(solution)/shard_map/ppermute | solution.py:29
  21.2 4.6 %collective-permute-start.2 = (bf16[18,1,768]{2,1,0:T(2,128)(2,1)}, bf16[18,1,768]{2,1,0:T(2,128)(2,1)}, u32[]{:S(2)}, u32[]{:S(2)}) collective-permute-start(bf16[18,1,768]{2,1,0:T(2,128)(2,1)} %get-tuple-element.69), channel_id=1, source_target_pairs={{0,1},{1,2},{2,3},{3,4},{4,5},{5,6},{6,7},{8,9},{9,10},{10,11},{11... | collective-permute-start | bytes 82952 | tf_op jit(solution)/shard_map/ppermute | solution.py:27
  33.5 20.7 %copy-start.1 = (bf16[768,768]{1,0:T(8,128)(2,1)S(1)}, bf16[768,768]{1,0:T(8,128)(2,1)}, u32[]{:S(2)}) copy-start(bf16[768,768]{1,0:T(8,128)(2,1)} %param.10) | copy-start | bytes 3538948
  78.0 112.4 %reduce-scatter.6.cloned.1.call-start = ((), (), s32[]{:S(2)}) async-start(), calls=%async_computation.2 | async-start | bytes 5308416 | tf_op jit(solution)/shard_map/reduce_scatter | solution.py:204
  83.7 138.8 %reduce-scatter.8.cloned.1.call-start = ((), (), s32[]{:S(2)}) async-start(), calls=%async_computation.4 | async-start | bytes 221184
  88.5 43.1 %copy-start.17 = (f32[2,4,768]{2,1,0:T(4,128)S(1)}, f32[2,4,768]{2,1,0:T(4,128)}, u32[]{:S(2)}) copy-start(f32[2,4,768]{2,1,0:T(4,128)} %copy-done.16) | copy-start | bytes 73732
  88.5 43.1 %copy-start.28 = (f32[2,4]{1,0:T(2,128)S(1)}, f32[2,4]{1,0:T(2,128)}, u32[]{:S(2)}) copy-start(f32[2,4]{1,0:T(2,128)} %copy-done.27) | copy-start | bytes 100
  88.5 43.0 %copy-start.30 = (f32[2,4]{1,0:T(2,128)S(1)}, f32[2,4]{1,0:T(2,128)}, u32[]{:S(2)}) copy-start(f32[2,4]{1,0:T(2,128)} %copy-done.29) | copy-start | bytes 100
  88.5 45.0 %copy-start.19 = (bf16[1,32,768]{2,1,0:T(8,128)(2,1)S(1)}, bf16[1,32,768]{2,1,0:T(8,128)(2,1)}, u32[]{:S(2)}) copy-start(bf16[1,32,768]{2,1,0:T(8,128)(2,1)} %copy-done.18) | copy-start | bytes 147460
  88.5 45.0 %copy-start.21 = (bf16[1,32,768]{2,1,0:T(8,128)(2,1)S(1)}, bf16[1,32,768]{2,1,0:T(8,128)(2,1)}, u32[]{:S(2)}) copy-start(bf16[1,32,768]{2,1,0:T(8,128)(2,1)} %copy-done.20) | copy-start | bytes 147460
  90.6 43.0 %copy-start.4 = (bf16[16,32,768]{2,1,0:T(8,128)(2,1)S(1)}, bf16[16,32,768]{2,1,0:T(8,128)(2,1)}, u32[]{:S(2)}) copy-start(bf16[16,32,768]{2,1,0:T(8,128)(2,1)} %param.7) | copy-start | bytes 2359300
  140.7 119.0 %all-gather.3.cloned.1.call-start = ((), (), s32[]{:S(2)}) async-start(), calls=%async_computation.3 | async-start | bytes 2949120 | tf_op jit(solution)/shard_map/all_gather | solution.py:15
  190.4 6.0 %collective-permute-start.5 = (bf16[1,32,768]{2,1,0:T(8,128)(2,1)S(1)}, bf16[1,32,768]{2,1,0:T(8,128)(2,1)S(1)}, u32[]{:S(2)}, u32[]{:S(2)}) collective-permute-start(bf16[1,32,768]{2,1,0:T(8,128)(2,1)S(1)} %get-tuple-element.71), channel_id=1, source_target_pairs={{8,0},{16,8},{24,16},{9,1},{17,9},{25,17},{10,2},{18,10},{26,18},{... | collective-permute-start | bytes 147464 | tf_op jit(solution)/shard_map/ppermute | solution.py:29
  191.7 6.3 %collective-permute-start.4 = (bf16[1,32,768]{2,1,0:T(8,128)(2,1)S(1)}, bf16[1,32,768]{2,1,0:T(8,128)(2,1)S(1)}, u32[]{:S(2)}, u32[]{:S(2)}) collective-permute-start(bf16[1,32,768]{2,1,0:T(8,128)(2,1)S(1)} %get-tuple-element.70), channel_id=1, source_target_pairs={{0,8},{8,16},{16,24},{1,9},{9,17},{17,25},{2,10},{10,18},{18,26},{... | collective-permute-start | bytes 147464 | tf_op jit(solution)/shard_map/ppermute | solution.py:27
  198.1 35.8 %collective-permute-start.7 = (bf16[18,1,768]{2,1,0:T(2,128)(2,1)S(1)}, bf16[18,1,768]{2,1,0:T(2,128)(2,1)S(1)}, u32[]{:S(2)}, u32[]{:S(2)}) collective-permute-start(bf16[18,1,768]{2,1,0:T(2,128)(2,1)S(1)} %get-tuple-element.67), channel_id=1, source_target_pairs={{1,0},{2,1},{3,2},{4,3},{5,4},{6,5},{7,6},{9,8},{10,9},{11,10},{12... | collective-permute-start | bytes 82952 | tf_op jit(solution)/shard_map/ppermute | solution.py:29
  199.4 34.5 %collective-permute-start.6 = (bf16[18,1,768]{2,1,0:T(2,128)(2,1)S(1)}, bf16[18,1,768]{2,1,0:T(2,128)(2,1)S(1)}, u32[]{:S(2)}, u32[]{:S(2)}) collective-permute-start(bf16[18,1,768]{2,1,0:T(2,128)(2,1)S(1)} %get-tuple-element.66), channel_id=1, source_target_pairs={{0,1},{1,2},{2,3},{3,4},{4,5},{5,6},{6,7},{8,9},{9,10},{10,11},{11... | collective-permute-start | bytes 82952 | tf_op jit(solution)/shard_map/ppermute | solution.py:27
  (21 other events, 38.5 us)
Sparse Core Ops, SparseCore 0:
  78.1 53.4 all-reduce.2
  133.9 56.4 reduce-scatter.5
  193.2 29.2 reduce-scatter.7
  224.2 35.4 all-gather.2
